TPU v7x, 32 devices: a whole 2x2x4 slice. The times are simulated.
32 devices in a mesh: fsdp: 2 (over x), ctx: 4 (over z), tp: 4 (over y, core).
Axes of the slice: x: 2, y: 2, z: 4, core: 2. Of those that a mesh axis runs over, the one named last changes fastest.
Arguments:
- tokens: bfloat16 [4, 1024, 2048], P('fsdp', 'ctx'), may hold values from -36 to 36
- cotangent: bfloat16 [4, 1024, 2048], P('fsdp', 'ctx'), may hold values from -9 to 9
- lengths: int32 [4, 2], P('fsdp'), may hold values from 1 to 768, 1024 in all within a row
- deal: int32 [4, 1024], P('fsdp'), may hold values from 0 to 1023, each once within a row
- att_proj: float32 [3, 2048, 2048], P(None, ('fsdp', 'ctx'), 'tp'), may hold values from -0.125 to 0.125
- attn_out: float32 [2048, 2048], P(('fsdp', 'ctx'), 'tp'), may hold values from -0.75 to 0.75
- ff_proj: float32 [2, 2048, 8192], P(None, ('fsdp', 'ctx'), 'tp'), may hold values from -0.125 to 0.125
- ff_out: float32 [2048, 8192], P(('fsdp', 'ctx'), 'tp'), may hold values from -0.0625 to 0.0625
- att_proj_first: float32 [3, 2048, 2048], P(None, ('fsdp', 'ctx'), 'tp')
- attn_out_first: float32 [2048, 2048], P(('fsdp', 'ctx'), 'tp')
- ff_proj_first: float32 [2, 2048, 8192], P(None, ('fsdp', 'ctx'), 'tp')
- ff_out_first: float32 [2048, 8192], P(('fsdp', 'ctx'), 'tp')
- att_proj_second: float32 [3, 2048, 2048], P(None, ('fsdp', 'ctx'), 'tp'), as said below
- attn_out_second: float32 [2048, 2048], P(('fsdp', 'ctx'), 'tp'), as said below
- ff_proj_second: float32 [2, 2048, 8192], P(None, ('fsdp', 'ctx'), 'tp'), as said below
- ff_out_second: float32 [2048, 8192], P(('fsdp', 'ctx'), 'tp'), as said below
Outputs:
- block_out: bfloat16 [4, 1024, 2048], P('fsdp', 'ctx')
- input_grad: float32 [4, 1024, 2048], P('fsdp', 'ctx')
- grad_norm: float32 [1], replicated
- att_proj_grad: float32 [3, 2048, 2048], P(None, ('fsdp', 'ctx'), 'tp')
- attn_out_grad: float32 [2048, 2048], P(('fsdp', 'ctx'), 'tp')
- ff_proj_grad: float32 [2, 2048, 8192], P(None, ('fsdp', 'ctx'), 'tp')
- ff_out_grad: float32 [2048, 8192], P(('fsdp', 'ctx'), 'tp')
- att_proj_first_new: float32 [3, 2048, 2048], P(None, ('fsdp', 'ctx'), 'tp')
- attn_out_first_new: float32 [2048, 2048], P(('fsdp', 'ctx'), 'tp')
- ff_proj_first_new: float32 [2, 2048, 8192], P(None, ('fsdp', 'ctx'), 'tp')
- ff_out_first_new: float32 [2048, 8192], P(('fsdp', 'ctx'), 'tp')
- att_proj_second_new: float32 [3, 2048, 2048], P(None, ('fsdp', 'ctx'), 'tp')
- attn_out_second_new: float32 [2048, 2048], P(('fsdp', 'ctx'), 'tp')
- ff_proj_second_new: float32 [2, 2048, 8192], P(None, ('fsdp', 'ctx'), 'tp')
- ff_out_second_new: float32 [2048, 8192], P(('fsdp', 'ctx'), 'tp')
- att_proj_new: float32 [3, 2048, 2048], P(None, ('fsdp', 'ctx'), 'tp')
- attn_out_new: float32 [2048, 2048], P(('fsdp', 'ctx'), 'tp')
- ff_proj_new: float32 [2, 2048, 8192], P(None, ('fsdp', 'ctx'), 'tp')
- ff_out_new: float32 [2048, 8192], P(('fsdp', 'ctx'), 'tp')
- att_proj_low: bfloat16 [3, 2048, 2048], P(None, ('fsdp', 'ctx'), 'tp')
- attn_out_low: bfloat16 [2048, 2048], P(('fsdp', 'ctx'), 'tp')
- ff_proj_low: bfloat16 [2, 2048, 8192], P(None, ('fsdp', 'ctx'), 'tp')
- ff_out_low: bfloat16 [2048, 8192], P(('fsdp', 'ctx'), 'tp')
Inputs may be any that keep to these rules, and one draw needn't show every extreme that they name: `lengths`: each row sums to 1024 and no entry exceeds 768. `deal`: each row is a permutation of the positions of its pack. `att_proj_second`: every entry is positive. `attn_out_second`: every entry is positive. `ff_proj_second`: every entry is positive. `ff_out_second`: every entry is positive.
All inputs are finite; a program needn't handle non-finite values.
Results may differ from a plain program's by a relative error of at most 0.017.
Values may be sent and summed in bfloat16 or wider, within the bound.
A program may use at most 320 MiB of HBM per device.

v0:
```python
import jax
import jax.numpy as jnp
from jax import lax
from jax.sharding import PartitionSpec as P

HEAD_DIM = 128
STEP = 10
EPS_NORM = 1e-05
BETA_ONE = 0.9
BETA_TWO = 0.95
EPS_ADAM = 1e-08
DECAY = 0.1
MAX_NORM = 1.0
NEG_FILL = -1e30
BF = jnp.bfloat16
F32 = jnp.float32


def mean_spread(values):
    centre = values - jnp.mean(values, axis=-1, keepdims=True)
    spread = jnp.mean(centre * centre, axis=-1, keepdims=True)
    scale = lax.rsqrt(spread + EPS_NORM)
    return (centre * scale, scale)


def norm_back(grad, normed, scale):
    return scale * (
        grad
        - jnp.mean(grad, axis=-1, keepdims=True)
        - normed * jnp.mean(grad * normed, axis=-1, keepdims=True)
    )


def dot(left, right, dims):
    return lax.dot_general(left, right, (dims, ((), ())), preferred_element_type=F32)


def adam_step(weight, grad_sum, first, second, clip_factor, learn_rate):
    clipped = grad_sum * clip_factor
    first_new = BETA_ONE * first + (1.0 - BETA_ONE) * clipped
    second_new = BETA_TWO * second + (1.0 - BETA_TWO) * clipped * clipped
    first_hat = first_new / (1.0 - BETA_ONE**STEP)
    second_hat = second_new / (1.0 - BETA_TWO**STEP)
    weight_new = weight - learn_rate * (
        first_hat / (jnp.sqrt(second_hat) + EPS_ADAM) + DECAY * weight
    )
    return (first_new, second_new, weight_new)


def make_shards(mesh):
    n_f, n_c, n_t = (mesh.shape[a] for a in ("fsdp", "ctx", "tp"))

    def by_ctx(block, shift):
        return lax.ppermute(block, "ctx", [(i, (i + shift) % n_c) for i in range(n_c)])

    def by_core(block):
        return lax.ppermute(block, "tp", [(i, i ^ 1) for i in range(n_t)])

    def by_pack(block, shift, other):
        pairs = [
            (f * n_t + t, (f + shift) % n_f * n_t + (t ^ 2 * other))
            for f in range(n_f)
            for t in range(n_t)
        ]
        return lax.ppermute(block, ("fsdp", "tp"), pairs)

    def gather_rows(half):
        mine = jnp.stack([half] + [by_ctx(half, s) for s in range(1, n_c)])
        both = jnp.stack([mine, by_core(mine)], axis=1)
        return both.reshape(-1, half.shape[1])

    def scatter_rows(partial):
        width = partial.shape[1]
        split = partial.astype(BF).reshape(n_c, 2, -1, width)
        summed = split[:, 0].astype(F32) + by_core(split[:, 1]).astype(F32)
        sent = summed.astype(BF)
        total = summed[0]
        for j in range(1, n_c):
            total = total + by_ctx(sent[j], -j).astype(F32)
        return total

    def gather_weight(shard):
        swapped = lax.all_to_all(shard.astype(BF), "ctx", 2, 1, tiled=True)
        columns = []
        for other in range(2):
            parts = [
                swapped if s == 0 and other == 0 else by_pack(swapped, s, other) for s in range(n_f)
            ]
            columns.append(jnp.concatenate(parts, axis=1))
        return jnp.concatenate(columns, axis=2)

    def scatter_grad(grad):
        count, height, width = grad.shape
        low = grad.astype(BF).reshape(count, n_f, height // n_f, 2, width // 2)
        total = grad.reshape(low.shape)[:, 0, :, 0]
        for other in range(2):
            for i in range(n_f):
                if i or other:
                    total = total + by_pack(low[:, i, :, other], -i, other).astype(F32)
        return lax.all_to_all(total.astype(BF), "ctx", 1, 2, tiled=True).astype(F32)

    def shards(
        tokens,
        cotangent,
        lengths,
        deal,
        att_proj,
        attn_out,
        ff_proj,
        ff_out,
        att_proj_first,
        attn_out_first,
        ff_proj_first,
        ff_out_first,
        att_proj_second,
        attn_out_second,
        ff_proj_second,
        ff_out_second,
    ):
        f_at, c_at, t_at = (lax.axis_index(a) for a in ("fsdp", "ctx", "tp"))
        pack_at, core_at = (t_at // 2, t_at % 2)
        packs, row_count, width = tokens.shape
        half = row_count // 2
        pack_len = deal.shape[1]
        score_scale = HEAD_DIM ** (-0.5)
        f_width = width // n_f

        def turned(rows):
            return jnp.concatenate(
                [
                    lax.dynamic_slice_in_dim(rows, (f_at - i) % n_f * f_width, f_width, 1)
                    for i in range(n_f)
                ],
                axis=1,
            )

        def own_rows(array):
            rows = array.reshape(packs * 2, half, width)
            return turned(lax.dynamic_index_in_dim(rows, t_at, 0, keepdims=False))

        own_tokens = own_rows(tokens)
        own_cot = own_rows(cotangent)
        att_w = gather_weight(jnp.concatenate([att_proj, attn_out[None]]))
        own_input = own_tokens.astype(F32)
        normed_one, scale_one = mean_spread(own_input)
        act_one = gather_rows(normed_one.astype(BF))
        deal_pack = lax.dynamic_index_in_dim(deal, pack_at, 0, keepdims=False)
        length_row = lax.dynamic_index_in_dim(lengths, pack_at, 0, keepdims=False)
        places = jnp.concatenate(
            [
                lax.dynamic_slice_in_dim(
                    deal_pack, (c_at - j) % n_c * row_count + (core_at + h) % 2 * half, half
                )
                for j in range(n_c)
                for h in range(2)
            ]
        )
        seqs = lengths.shape[1]
        before = jnp.arange(seqs)[:, None] > jnp.arange(seqs)[None, :]
        starts = jnp.sum(jnp.where(before, length_row[None, :], 0), axis=1)
        inside = (places[:, None] >= starts[None, :]) & (
            places[:, None] < (starts + length_row)[None, :]
        )
        firsts = jnp.sum(jnp.where(inside, starts[None, :], 0), axis=1)
        allowed = (places[None, :] <= places[:, None]) & (places[None, :] >= firsts[:, None])
        freq_steps = jnp.arange(HEAD_DIM // 2, dtype=F32)
        inverse = jnp.power(10000.0, -2.0 * freq_steps / HEAD_DIM)
        angles = (places - firsts).astype(F32)[:, None] * inverse[None, :]
        cos_table, sine_table = (jnp.cos(angles), jnp.sin(angles))

        def turn(values, sign):
            low, high = (values[..., : HEAD_DIM // 2], values[..., HEAD_DIM // 2 :])
            sine = sign * sine_table[:, None, :]
            cos = cos_table[:, None, :]
            return jnp.concatenate([low * cos - high * sine, high * cos + low * sine], axis=-1)

        rank_width = att_w.shape[2]
        heads = rank_width // HEAD_DIM
        raw = [
            dot(act_one, att_w[i], ((1,), (0,))).reshape(pack_len, heads, HEAD_DIM)
            for i in range(3)
        ]
        query = turn(raw[0], 1.0).astype(BF)
        key = turn(raw[1], 1.0).astype(BF)
        value = raw[2].astype(BF)
        scores = jnp.einsum("thd,khd->htk", query, key, preferred_element_type=F32) * score_scale
        scores = jnp.where(allowed[None], scores, NEG_FILL)
        exp_scores = jnp.exp(scores - jnp.max(scores, axis=2, keepdims=True))
        probs = exp_scores / jnp.sum(exp_scores, axis=2, keepdims=True)
        probs_low = probs.astype(BF)
        attended = jnp.einsum("htk,khd->thd", probs_low, value, preferred_element_type=F32)
        attended_low = attended.reshape(pack_len, rank_width).astype(BF)
        out_part = dot(attended_low, att_w[3], ((1,), (1,)))
        resid_mid = own_input + scatter_rows(out_part)
        normed_two, scale_two = mean_spread(resid_mid)
        act_two = gather_rows(normed_two.astype(BF))
        ff_w = gather_weight(jnp.concatenate([ff_proj, ff_out[None]]))
        cot_rows = gather_rows(own_cot)
        up = dot(act_two, ff_w[0], ((1,), (0,)))
        gate = dot(act_two, ff_w[1], ((1,), (0,)))
        sigma = jax.nn.sigmoid(gate)
        hidden_low = (gate * sigma * up).astype(BF)
        hidden_grad = dot(cot_rows, ff_w[2], ((1,), (0,)))
        up_grad = (hidden_grad * gate * sigma).astype(BF)
        gate_grad = (hidden_grad * up * sigma * (1.0 + gate * (1.0 - sigma))).astype(BF)
        act_two_part = dot(up_grad, ff_w[0], ((1,), (1,))) + dot(gate_grad, ff_w[1], ((1,), (1,)))
        act_two_grad = scatter_rows(act_two_part)
        mid_grad = own_cot.astype(F32) + norm_back(act_two_grad, normed_two, scale_two)
        mid_rows = gather_rows(mid_grad.astype(BF))
        ff_branch = scatter_rows(dot(hidden_low, ff_w[2], ((1,), (1,))))
        block_rows = turned((resid_mid + ff_branch).astype(BF))
        block_out = lax.all_gather(block_rows, "tp", axis=0, tiled=True)
        ff_grad = jnp.stack(
            [
                dot(act_two, up_grad, ((0,), (0,))),
                dot(act_two, gate_grad, ((0,), (0,))),
                dot(cot_rows, hidden_low, ((0,), (0,))),
            ]
        )
        ff_total = scatter_grad(ff_grad)
        attended_grad = dot(mid_rows, att_w[3], ((1,), (0,))).astype(BF)
        attended_grad = attended_grad.reshape(pack_len, heads, HEAD_DIM)
        value_grad = jnp.einsum(
            "htk,thd->khd", probs_low, attended_grad, preferred_element_type=F32
        )
        prob_grad = jnp.einsum("thd,khd->htk", attended_grad, value, preferred_element_type=F32)
        delta_rows = jnp.sum(probs * prob_grad, axis=2, keepdims=True)
        score_grad = (probs * (prob_grad - delta_rows)).astype(BF)
        query_grad = (
            jnp.einsum("htk,khd->thd", score_grad, key, preferred_element_type=F32) * score_scale
        )
        key_grad = (
            jnp.einsum("htk,thd->khd", score_grad, query, preferred_element_type=F32) * score_scale
        )
        joint_grad = [
            part.reshape(pack_len, rank_width).astype(BF)
            for part in (turn(query_grad, -1.0), turn(key_grad, -1.0), value_grad)
        ]
        act_one_part = sum((dot(joint_grad[i], att_w[i], ((1,), (1,))) for i in range(3)))
        act_one_grad = scatter_rows(act_one_part)
        input_rows = turned(norm_back(act_one_grad, normed_one, scale_one) + mid_grad)
        input_grad = lax.all_gather(input_rows, "tp", axis=0, tiled=True)
        att_grad = jnp.stack(
            [dot(act_one, part, ((0,), (0,))) for part in joint_grad]
            + [dot(mid_rows, attended_low, ((0,), (0,)))]
        )
        att_total = scatter_grad(att_grad)
        square_sum = lax.psum(
            jnp.sum(att_total * att_total) + jnp.sum(ff_total * ff_total), ("fsdp", "ctx", "tp")
        )
        norm_value = jnp.sqrt(square_sum)
        clip_factor = jnp.minimum(1.0, MAX_NORM / (norm_value + 1e-06))
        base_rate = width ** (-0.5)
        out_rate = (width // 32) ** (-0.5)
        grads = (att_total[:3], att_total[3], ff_total[:2], ff_total[2])
        weights = (att_proj, attn_out, ff_proj, ff_out)
        firsts_old = (att_proj_first, attn_out_first, ff_proj_first, ff_out_first)
        seconds_old = (att_proj_second, attn_out_second, ff_proj_second, ff_out_second)
        rates = (base_rate, out_rate, base_rate, base_rate)
        news = [
            adam_step(w, g, m, v, clip_factor, r)
            for w, g, m, v, r in zip(weights, grads, firsts_old, seconds_old, rates)
        ]
        return (
            block_out.reshape(tokens.shape),
            input_grad.reshape(tokens.shape),
            norm_value.reshape(1),
            *grads,
            *(n[0] for n in news),
            *(n[1] for n in news),
            *(n[2] for n in news),
            *(n[2].astype(BF) for n in news),
        )

    return shards


def solution(mesh):
    act = P("fsdp", "ctx", None)
    table = P("fsdp", None)
    cube = P(None, ("fsdp", "ctx"), "tp")
    flat = P(("fsdp", "ctx"), "tp")
    group = (cube, flat, cube, flat)
    in_specs = (act, act, table, table) + group * 3
    out_specs = (act, act, P()) + group * 5
    return jax.shard_map(
        make_shards(mesh), mesh=mesh, in_specs=in_specs, out_specs=out_specs, check_vma=False
    )
```

profile of v0, /device:TPU:0, one launch (start us, length us, event | category | flops | bytes accessed | tf_op | source)
XLA Modules:
  0.0 1239.6 jit_solution(7783477940593059198)
XLA Ops:
  28.0 44.8 %collective-permute-done.1 = bf16[128,2048]{1,0:T(8,128)(2,1)} collective-permute-done((bf16[128,2048]{1,0:T(8,128)(2,1)}, bf16[128,2048]{1,0:T(8,128)(2,1)}, u32[]{:S(2)}, u32[]{:S(2)}) %collective-permute-start.1) | collective-permute-done | bytes 524320 | tf_op jit(solution)/shard_map/ppermute | solution.py:54
  93.8 17.7 %collective-permute-done.6 = bf16[4,1024,128]{1,2,0:T(8,128)(2,1)S(1)} collective-permute-done((bf16[4,1024,128]{1,2,0:T(8,128)(2,1)S(1)}, bf16[4,1024,128]{1,2,0:T(8,128)(2,1)S(1)}, u32[]{:S(2)}, u32[]{:S(2)}) %collective-permute-start.6) | collective-permute-done | bytes 1048608 | tf_op jit(solution)/shard_map/ppermute | solution.py:65
  111.4 20.4 %collective-permute-done.5 = bf16[4,1024,128]{1,2,0:T(8,128)(2,1)S(1)} collective-permute-done((bf16[4,1024,128]{1,2,0:T(8,128)(2,1)S(1)}, bf16[4,1024,128]{1,2,0:T(8,128)(2,1)S(1)}, u32[]{:S(2)}, u32[]{:S(2)}) %collective-permute-start.5) | collective-permute-done | bytes 1048608 | tf_op jit(solution)/shard_map/ppermute | solution.py:65
  189.7 71.6 %collective-permute-done.10 = bf16[128,2048]{1,0:T(8,128)(2,1)S(1)} collective-permute-done((bf16[128,2048]{1,0:T(8,128)(2,1)S(1)}, bf16[128,2048]{1,0:T(8,128)(2,1)S(1)}, u32[]{:S(2)}, u32[]{:S(2)}) %collective-permute-start.10) | collective-permute-done | bytes 524320 | tf_op jit(solution)/shard_map/ppermute | solution.py:54
  261.3 65.1 %collective-permute-start.22 = (bf16[128,2048]{1,0:T(8,128)(2,1)S(1)}, bf16[128,2048]{1,0:T(8,128)(2,1)S(1)}, u32[]{:S(2)}, u32[]{:S(2)}) collective-permute-start(bf16[128,2048]{1,0:T(8,128)(2,1)S(1)} %get-tuple-element.108), channel_id=1, source_target_pairs={{0,4},{4,8},{8,12},{12,0},{1,5},{5,9},{9,13},{13,1},{2,6},{6,10},{... | collective-permute-start | bytes 1572872 | tf_op jit(solution)/shard_map/ppermute | solution.py:54
  329.5 12.8 %collective-permute-start.13 = (bf16[128,2048]{1,0:T(8,128)(2,1)}, bf16[128,2048]{1,0:T(8,128)(2,1)}, u32[]{:S(2)}, u32[]{:S(2)}) collective-permute-start(bf16[128,2048]{1,0:T(8,128)(2,1)} %fusion.76), channel_id=1, source_target_pairs={{0,12},{4,0},{8,4},{12,8},{1,13},{5,1},{9,5},{13,9},{2,14},{6,2},{... | collective-permute-start | bytes 1572872 | tf_op jit(solution)/shard_map/ppermute | solution.py:54
  342.8 8.0 collective-permute-start.11
  350.8 33.1 %collective-permute-done.23 = bf16[128,2048]{1,0:T(8,128)(2,1)S(1)} collective-permute-done((bf16[128,2048]{1,0:T(8,128)(2,1)S(1)}, bf16[128,2048]{1,0:T(8,128)(2,1)S(1)}, u32[]{:S(2)}, u32[]{:S(2)}) %collective-permute-start.23) | collective-permute-done | bytes 524320 | tf_op jit(solution)/shard_map/ppermute | solution.py:54
  397.7 8.1 collective-permute-done.12
  415.5 7.8 reshape.558
  423.3 11.2 copy.390
  451.4 15.5 %collective-permute-done.17 = bf16[3,1024,512]{2,1,0:T(8,128)(2,1)} collective-permute-done((bf16[3,1024,512]{2,1,0:T(8,128)(2,1)}, bf16[3,1024,512]{2,1,0:T(8,128)(2,1)}, u32[]{:S(2)}, u32[]{:S(2)}) %collective-permute-start.17) | collective-permute-done | bytes 3145760 | tf_op jit(solution)/shard_map/ppermute | solution.py:65
  466.9 67.0 %collective-permute-done.16 = bf16[3,1024,512]{2,1,0:T(8,128)(2,1)} collective-permute-done((bf16[3,1024,512]{2,1,0:T(8,128)(2,1)}, bf16[3,1024,512]{2,1,0:T(8,128)(2,1)}, u32[]{:S(2)}, u32[]{:S(2)}) %collective-permute-start.16) | collective-permute-done | bytes 3145760 | tf_op jit(solution)/shard_map/ppermute | solution.py:65
  533.8 14.6 %maximum_maximum_fusion = bf16[3,2048,1024]{2,1,0:T(8,128)(2,1)S(1)} fusion(bf16[3,1024,512]{2,1,0:T(8,128)(2,1)} %collective-permute-done.17, bf16[3,1024,512]{2,1,0:T(8,128)(2,1)} %collective-permute-done.16, bf16[3,1024,512]{2,1,0:T(8,128)(2,1)} %collective-permute-done.15, bf16[3,1024,512]{2,1,0:T(8,128)(2,1)} %bitcast.502), kind=kLoop, calls=%fused_computation.2 | loop fusion | flops 50331648 | bytes 25165824 | tf_op jit(solution)/shard_map/concatenate | solution.py:90
  566.9 14.0 %fusion.12 = (bf16[1024,1024]{1,0:T(8,128)(2,1)}, bf16[1024,1024]{1,0:T(8,128)(2,1)}, bf16[1024,1024]{1,0:T(8,128)(2,1)}, f32[1024,1024]{0,1:T(8,128)}) fusion(f32[1024,1024]{0,1:T(8,128)} %fusion.23, f32[1024,1024]{0,1:T(8,128)} %fusion.22, bf16[1024,2048]{1,0:T(8,128)(2,1)} %bitcast.482, bf16[3,2048,1024]{2,1,0:T(8,128)(2,1)} %copy-done.14), kind=kOutput, calls=%fused_computation.43 | convolution fusion | flops 4311744512 | bytes 27262976 | tf_op jit(solution)/shard_map/dot_general | solution.py:35
  591.7 9.3 convolution_convert_fusion.1
  601.0 10.3 fusion.20
  611.3 11.6 add_convert_fusion.1
  649.8 10.0 collective-permute-done.29
  659.7 22.3 %collective-permute-done.28 = bf16[128,2048]{1,0:T(8,128)(2,1)} collective-permute-done((bf16[128,2048]{1,0:T(8,128)(2,1)}, bf16[128,2048]{1,0:T(8,128)(2,1)}, u32[]{:S(2)}, u32[]{:S(2)}) %collective-permute-start.28) | collective-permute-done | bytes 524320 | tf_op jit(solution)/shard_map/ppermute | solution.py:54
  683.9 9.5 collective-permute-done.21
  693.4 32.7 %collective-permute-done.20 = bf16[128,2048]{1,0:T(8,128)(2,1)S(1)} collective-permute-done((bf16[128,2048]{1,0:T(8,128)(2,1)S(1)}, bf16[128,2048]{1,0:T(8,128)(2,1)S(1)}, u32[]{:S(2)}, u32[]{:S(2)}) %collective-permute-start.20) | collective-permute-done | bytes 524320 | tf_op jit(solution)/shard_map/ppermute | solution.py:54
  726.9 11.0 collective-permute-start.32
  750.4 33.8 %collective-permute-done.31 = bf16[128,2048]{1,0:T(8,128)(2,1)S(1)} collective-permute-done((bf16[128,2048]{1,0:T(8,128)(2,1)S(1)}, bf16[128,2048]{1,0:T(8,128)(2,1)S(1)}, u32[]{:S(2)}, u32[]{:S(2)}) %collective-permute-start.31) | collective-permute-done | bytes 524320 | tf_op jit(solution)/shard_map/ppermute | solution.py:54
  799.4 12.5 %pad_maximum_fusion = f32[3,2,1024,2,512]{4,2,3,1,0:T(8,128)} fusion(f32[1,2,1024,2,512]{4,2,3,1,0:T(8,128)} %convolution_bitcast_fusion, f32[1,2,1024,2,512]{4,2,3,1,0:T(8,128)S(1)} %convolution_bitcast_fusion.1, f32[1,2,1024,2,512]{4,2,3,1,0:T(8,128)S(1)} %convolution_bitcast_fusion.2), kind=kLoop, calls=%fused_computation.1 | loop fusion | flops 12582912 | bytes 50331648 | tf_op jit(solution)/shard_map/stack | solution.py:213
  845.0 23.0 %collective-permute-done.43 = bf16[3,1024,512]{2,1,0:T(8,128)(2,1)} collective-permute-done((bf16[3,1024,512]{2,1,0:T(8,128)(2,1)}, bf16[3,1024,512]{2,1,0:T(8,128)(2,1)}, u32[]{:S(2)}, u32[]{:S(2)}) %collective-permute-start.43) | collective-permute-done | bytes 3145760 | tf_op jit(solution)/shard_map/ppermute | solution.py:65
  868.1 78.2 %collective-permute-done.42 = bf16[3,1024,512]{2,1,0:T(8,128)(2,1)} collective-permute-done((bf16[3,1024,512]{2,1,0:T(8,128)(2,1)}, bf16[3,1024,512]{2,1,0:T(8,128)(2,1)}, u32[]{:S(2)}, u32[]{:S(2)}) %collective-permute-start.42) | collective-permute-done | bytes 3145760 | tf_op jit(solution)/shard_map/ppermute | solution.py:65
  946.3 7.2 fusion.5
  994.9 52.5 %collective-permute-done.37 = bf16[128,2048]{1,0:T(8,128)(2,1)S(1)} collective-permute-done((bf16[128,2048]{1,0:T(8,128)(2,1)S(1)}, bf16[128,2048]{1,0:T(8,128)(2,1)S(1)}, u32[]{:S(2)}, u32[]{:S(2)}) %collective-permute-start.37) | collective-permute-done | bytes 524320 | tf_op jit(solution)/shard_map/ppermute | solution.py:54
  1048.9 42.4 %collective-permute-done.36 = bf16[128,2048]{1,0:T(8,128)(2,1)S(1)} collective-permute-done((bf16[128,2048]{1,0:T(8,128)(2,1)S(1)}, bf16[128,2048]{1,0:T(8,128)(2,1)S(1)}, u32[]{:S(2)}, u32[]{:S(2)}) %collective-permute-start.36) | collective-permute-done | bytes 524320 | tf_op jit(solution)/shard_map/ppermute | solution.py:54
  1100.9 20.4 %all-to-all-start.2 = ((bf16[4,1024,128]{2,0,1:T(4,128)(2,1)}), bf16[4,1024,128]{2,0,1:T(4,128)(2,1)S(1)}, u32[]{:S(2)}, u32[]{:S(2)}) async-start(bf16[4,1024,128]{2,0,1:T(4,128)(2,1)} %copy.371), calls=%async_computation.2 | async-start | bytes 2097152 | tf_op jit(solution)/shard_map/all_to_all | solution.py:100
  1158.8 40.1 %psum.7 = f32[]{:T(128)} all-reduce(f32[]{:T(128)S(6)} %add.425), channel_id=1, replica_groups=mesh['fsdp'=2,'ctx'=4,'tp'=4] {'fsdp','ctx','tp'}, use_global_device_ids=true, to_apply=%region_15.16 | all-reduce | flops 1 | bytes 8 | tf_op jit(solution)/shard_map/psum | solution.py:248
  (382 shorter events, 382.1 us)
Async XLA Ops:
  15.3 57.5 %collective-permute-start.1 = (bf16[128,2048]{1,0:T(8,128)(2,1)}, bf16[128,2048]{1,0:T(8,128)(2,1)}, u32[]{:S(2)}, u32[]{:S(2)}) collective-permute-start(bf16[128,2048]{1,0:T(8,128)(2,1)} %fusion.49), channel_id=1, source_target_pairs={{0,8},{4,12},{8,0},{12,4},{1,9},{5,13},{9,1},{13,5},{2,10},{6,14},... | collective-permute-start | bytes 1572872 | tf_op jit(solution)/shard_map/ppermute | solution.py:54
  15.3 57.5 %collective-permute-start = (bf16[128,2048]{1,0:T(8,128)(2,1)}, bf16[128,2048]{1,0:T(8,128)(2,1)}, u32[]{:S(2)}, u32[]{:S(2)}) collective-permute-start(bf16[128,2048]{1,0:T(8,128)(2,1)} %fusion.49), channel_id=1, source_target_pairs={{0,4},{4,8},{8,12},{12,0},{1,5},{5,9},{9,13},{13,1},{2,6},{6,10},{... | collective-permute-start | bytes 1572872 | tf_op jit(solution)/shard_map/ppermute | solution.py:54
  19.0 63.7 %all-to-all-start = ((bf16[4,256,512]{1,0,2:T(4,128)(2,1)}), bf16[4,256,512]{1,0,2:T(4,128)(2,1)S(1)}, u32[]{:S(2)}, u32[]{:S(2)}) async-start(bf16[4,256,512]{1,0,2:T(4,128)(2,1)} %copy.331), calls=%async_computation | async-start | bytes 2097152 | tf_op jit(solution)/shard_map/all_to_all | solution.py:83
  171.8 213.8 %all-to-all-start.1 = ((bf16[3,256,2048]{1,0,2:T(4,128)(2,1)}), bf16[3,256,2048]{1,0,2:T(4,128)(2,1)}, u32[]{:S(2)}, u32[]{:S(2)}) async-start(bf16[3,256,2048]{1,0,2:T(4,128)(2,1)} %pad_maximum_fusion.4), calls=%async_computation.1 | async-start | bytes 8388608 | tf_op jit(solution)/shard_map/all_to_all | solution.py:83
  177.0 944.3 %all-gather.3.cloned.1.call-start = ((), (), s32[]{:S(2)}) async-start(), calls=%async_computation.4 | async-start | bytes 2621440 | tf_op jit(solution)/shard_map/all_gather | solution.py:212
  180.3 81.0 %collective-permute-start.10 = (bf16[128,2048]{1,0:T(8,128)(2,1)S(1)}, bf16[128,2048]{1,0:T(8,128)(2,1)S(1)}, u32[]{:S(2)}, u32[]{:S(2)}) collective-permute-start(bf16[128,2048]{1,0:T(8,128)(2,1)S(1)} %get-tuple-element.88), channel_id=1, source_target_pairs={{0,4},{4,8},{8,12},{12,0},{1,5},{5,9},{9,13},{13,1},{2,6},{6,10},{... | collective-permute-start | bytes 1572872 | tf_op jit(solution)/shard_map/ppermute | solution.py:54
  182.4 145.3 %collective-permute-start.9 = (bf16[128,2048]{1,0:T(8,128)(2,1)S(1)}, bf16[128,2048]{1,0:T(8,128)(2,1)S(1)}, u32[]{:S(2)}, u32[]{:S(2)}) collective-permute-start(bf16[128,2048]{1,0:T(8,128)(2,1)S(1)} %get-tuple-element.89), channel_id=1, source_target_pairs={{0,8},{4,12},{8,0},{12,4},{1,9},{5,13},{9,1},{13,5},{2,10},{6,14},... | collective-permute-start | bytes 1572872 | tf_op jit(solution)/shard_map/ppermute | solution.py:54
  184.8 143.0 %collective-permute-start.8 = (bf16[128,2048]{1,0:T(8,128)(2,1)S(1)}, bf16[128,2048]{1,0:T(8,128)(2,1)S(1)}, u32[]{:S(2)}, u32[]{:S(2)}) collective-permute-start(bf16[128,2048]{1,0:T(8,128)(2,1)S(1)} %get-tuple-element.87), channel_id=1, source_target_pairs={{0,12},{4,0},{8,4},{12,8},{1,13},{5,1},{9,5},{13,9},{2,14},{6,2},{... | collective-permute-start | bytes 1572872 | tf_op jit(solution)/shard_map/ppermute | solution.py:54
  187.6 155.2 %collective-permute-start.24 = (bf16[128,2048]{1,0:T(8,128)(2,1)S(1)}, bf16[128,2048]{1,0:T(8,128)(2,1)S(1)}, u32[]{:S(2)}, u32[]{:S(2)}) collective-permute-start(bf16[128,2048]{1,0:T(8,128)(2,1)S(1)} %get-tuple-element.108), channel_id=1, source_target_pairs={{0,12},{4,0},{8,4},{12,8},{1,13},{5,1},{9,5},{13,9},{2,14},{6,2},{... | collective-permute-start | bytes 1572872 | tf_op jit(solution)/shard_map/ppermute | solution.py:54
  188.2 195.7 %collective-permute-start.23 = (bf16[128,2048]{1,0:T(8,128)(2,1)S(1)}, bf16[128,2048]{1,0:T(8,128)(2,1)S(1)}, u32[]{:S(2)}, u32[]{:S(2)}) collective-permute-start(bf16[128,2048]{1,0:T(8,128)(2,1)S(1)} %get-tuple-element.108), channel_id=1, source_target_pairs={{0,8},{4,12},{8,0},{12,4},{1,9},{5,13},{9,1},{13,5},{2,10},{6,14},... | collective-permute-start | bytes 1572872 | tf_op jit(solution)/shard_map/ppermute | solution.py:54
  261.3 122.6 %collective-permute-start.22 = (bf16[128,2048]{1,0:T(8,128)(2,1)S(1)}, bf16[128,2048]{1,0:T(8,128)(2,1)S(1)}, u32[]{:S(2)}, u32[]{:S(2)}) collective-permute-start(bf16[128,2048]{1,0:T(8,128)(2,1)S(1)} %get-tuple-element.108), channel_id=1, source_target_pairs={{0,4},{4,8},{8,12},{12,0},{1,5},{5,9},{9,13},{13,1},{2,6},{6,10},{... | collective-permute-start | bytes 1572872 | tf_op jit(solution)/shard_map/ppermute | solution.py:54
  329.5 66.8 %collective-permute-start.13 = (bf16[128,2048]{1,0:T(8,128)(2,1)}, bf16[128,2048]{1,0:T(8,128)(2,1)}, u32[]{:S(2)}, u32[]{:S(2)}) collective-permute-start(bf16[128,2048]{1,0:T(8,128)(2,1)} %fusion.76), channel_id=1, source_target_pairs={{0,12},{4,0},{8,4},{12,8},{1,13},{5,1},{9,5},{13,9},{2,14},{6,2},{... | collective-permute-start | bytes 1572872 | tf_op jit(solution)/shard_map/ppermute | solution.py:54
  342.3 63.5 %collective-permute-start.12 = (bf16[128,2048]{1,0:T(8,128)(2,1)}, bf16[128,2048]{1,0:T(8,128)(2,1)}, u32[]{:S(2)}, u32[]{:S(2)}) collective-permute-start(bf16[128,2048]{1,0:T(8,128)(2,1)} %fusion.76), channel_id=1, source_target_pairs={{0,8},{4,12},{8,0},{12,4},{1,9},{5,13},{9,1},{13,5},{2,10},{6,14},... | collective-permute-start | bytes 1572872 | tf_op jit(solution)/shard_map/ppermute | solution.py:54
  342.8 64.7 %collective-permute-start.11 = (bf16[128,2048]{1,0:T(8,128)(2,1)}, bf16[128,2048]{1,0:T(8,128)(2,1)}, u32[]{:S(2)}, u32[]{:S(2)}) collective-permute-start(bf16[128,2048]{1,0:T(8,128)(2,1)} %fusion.76), channel_id=1, source_target_pairs={{0,4},{4,8},{8,12},{12,0},{1,5},{5,9},{9,13},{13,1},{2,6},{6,10},{... | collective-permute-start | bytes 1572872 | tf_op jit(solution)/shard_map/ppermute | solution.py:54
  394.7 72.2 %collective-permute-start.17 = (bf16[3,1024,512]{2,1,0:T(8,128)(2,1)}, bf16[3,1024,512]{2,1,0:T(8,128)(2,1)}, u32[]{:S(2)}, u32[]{:S(2)}) collective-permute-start(bf16[3,1024,512]{2,1,0:T(8,128)(2,1)} %bitcast.499), channel_id=1, source_target_pairs={{0,18},{1,19},{2,16},{3,17},{16,2},{17,3},{18,0},{19,1},{4,22},{5,... | collective-permute-start | bytes 9437192 | tf_op jit(solution)/shard_map/ppermute | solution.py:65
  396.3 137.5 %collective-permute-start.16 = (bf16[3,1024,512]{2,1,0:T(8,128)(2,1)}, bf16[3,1024,512]{2,1,0:T(8,128)(2,1)}, u32[]{:S(2)}, u32[]{:S(2)}) collective-permute-start(bf16[3,1024,512]{2,1,0:T(8,128)(2,1)} %bitcast.500), channel_id=1, source_target_pairs={{0,2},{1,3},{2,0},{3,1},{16,18},{17,19},{18,16},{19,17},{4,6},{5,7... | collective-permute-start | bytes 9437192 | tf_op jit(solution)/shard_map/ppermute | solution.py:65
  405.8 128.1 %collective-permute-start.15 = (bf16[3,1024,512]{2,1,0:T(8,128)(2,1)}, bf16[3,1024,512]{2,1,0:T(8,128)(2,1)}, u32[]{:S(2)}, u32[]{:S(2)}) collective-permute-start(bf16[3,1024,512]{2,1,0:T(8,128)(2,1)} %bitcast.501), channel_id=1, source_target_pairs={{0,16},{1,17},{2,18},{3,19},{16,0},{17,1},{18,2},{19,3},{4,20},{5,... | collective-permute-start | bytes 9437192 | tf_op jit(solution)/shard_map/ppermute | solution.py:65
  648.2 77.9 %collective-permute-start.20 = (bf16[128,2048]{1,0:T(8,128)(2,1)S(1)}, bf16[128,2048]{1,0:T(8,128)(2,1)S(1)}, u32[]{:S(2)}, u32[]{:S(2)}) collective-permute-start(bf16[128,2048]{1,0:T(8,128)(2,1)S(1)} %get-tuple-element.84), channel_id=1, source_target_pairs={{0,8},{4,12},{8,0},{12,4},{1,9},{5,13},{9,1},{13,5},{2,10},{6,14},... | collective-permute-start | bytes 1572872 | tf_op jit(solution)/shard_map/ppermute | solution.py:54
  659.7 66.4 %collective-permute-start.19 = (bf16[128,2048]{1,0:T(8,128)(2,1)S(1)}, bf16[128,2048]{1,0:T(8,128)(2,1)S(1)}, u32[]{:S(2)}, u32[]{:S(2)}) collective-permute-start(bf16[128,2048]{1,0:T(8,128)(2,1)S(1)} %get-tuple-element.82), channel_id=1, source_target_pairs={{0,12},{4,0},{8,4},{12,8},{1,13},{5,1},{9,5},{13,9},{2,14},{6,2},{... | collective-permute-start | bytes 1572872 | tf_op jit(solution)/shard_map/ppermute | solution.py:54
  795.9 72.2 %collective-permute-start.43 = (bf16[3,1024,512]{2,1,0:T(8,128)(2,1)}, bf16[3,1024,512]{2,1,0:T(8,128)(2,1)}, u32[]{:S(2)}, u32[]{:S(2)}) collective-permute-start(bf16[3,1024,512]{2,1,0:T(8,128)(2,1)} %get-tuple-element.51), channel_id=1, source_target_pairs={{0,18},{1,19},{2,16},{3,17},{16,2},{17,3},{18,0},{19,1},{4,22},{5,... | collective-permute-start | bytes 9437192 | tf_op jit(solution)/shard_map/ppermute | solution.py:65
  797.6 148.7 %collective-permute-start.42 = (bf16[3,1024,512]{2,1,0:T(8,128)(2,1)}, bf16[3,1024,512]{2,1,0:T(8,128)(2,1)}, u32[]{:S(2)}, u32[]{:S(2)}) collective-permute-start(bf16[3,1024,512]{2,1,0:T(8,128)(2,1)} %get-tuple-element.52), channel_id=1, source_target_pairs={{0,2},{1,3},{2,0},{3,1},{16,18},{17,19},{18,16},{19,17},{4,6},{5,7... | collective-permute-start | bytes 9437192 | tf_op jit(solution)/shard_map/ppermute | solution.py:65
  798.9 147.4 %collective-permute-start.41 = (bf16[3,1024,512]{2,1,0:T(8,128)(2,1)}, bf16[3,1024,512]{2,1,0:T(8,128)(2,1)}, u32[]{:S(2)}, u32[]{:S(2)}) collective-permute-start(bf16[3,1024,512]{2,1,0:T(8,128)(2,1)} %get-tuple-element.50), channel_id=1, source_target_pairs={{0,16},{1,17},{2,18},{3,19},{16,0},{17,1},{18,2},{19,3},{4,20},{5,... | collective-permute-start | bytes 9437192 | tf_op jit(solution)/shard_map/ppermute | solution.py:65
  845.0 135.0 %collective-permute-start.34 = (bf16[4,128,2048]{2,1,0:T(8,128)(2,1)}, bf16[4,128,2048]{2,1,0:T(8,128)(2,1)}, u32[]{:S(2)}, u32[]{:S(2)}) collective-permute-start(bf16[4,128,2048]{2,1,0:T(8,128)(2,1)} %slice_bitcast_fusion.14), channel_id=1, source_target_pairs={{0,1},{1,0},{2,3},{3,2},{4,5},{5,4},{6,7},{7,6},{8,9},{9,8},{10,11... | collective-permute-start | bytes 6291464 | tf_op jit(solution)/shard_map/ppermute | solution.py:57
  958.2 142.7 %all-to-all-start.3 = ((bf16[3,1024,512]{2,0,1:T(4,128)(2,1)}), bf16[3,1024,512]{2,0,1:T(4,128)(2,1)}, u32[]{:S(2)}, u32[]{:S(2)}) async-start(bf16[3,1024,512]{2,0,1:T(4,128)(2,1)} %copy.377), calls=%async_computation.3 | async-start | bytes 8388608 | tf_op jit(solution)/shard_map/all_to_all | solution.py:100
  963.1 263.3 %all-gather.5.cloned.1.call-start = ((), (), s32[]{:S(2)}) async-start(), calls=%async_computation.5 | async-start | bytes 5242880 | tf_op jit(solution)/shard_map/all_gather | solution.py:242
  983.4 64.0 %collective-permute-start.37 = (bf16[128,2048]{1,0:T(8,128)(2,1)S(1)}, bf16[128,2048]{1,0:T(8,128)(2,1)S(1)}, u32[]{:S(2)}, u32[]{:S(2)}) collective-permute-start(bf16[128,2048]{1,0:T(8,128)(2,1)S(1)} %get-tuple-element.71), channel_id=1, source_target_pairs={{0,4},{4,8},{8,12},{12,0},{1,5},{5,9},{9,13},{13,1},{2,6},{6,10},{... | collective-permute-start | bytes 1572872 | tf_op jit(solution)/shard_map/ppermute | solution.py:54
  985.3 105.9 %collective-permute-start.36 = (bf16[128,2048]{1,0:T(8,128)(2,1)S(1)}, bf16[128,2048]{1,0:T(8,128)(2,1)S(1)}, u32[]{:S(2)}, u32[]{:S(2)}) collective-permute-start(bf16[128,2048]{1,0:T(8,128)(2,1)S(1)} %get-tuple-element.72), channel_id=1, source_target_pairs={{0,8},{4,12},{8,0},{12,4},{1,9},{5,13},{9,1},{13,5},{2,10},{6,14},... | collective-permute-start | bytes 1572872 | tf_op jit(solution)/shard_map/ppermute | solution.py:54
  987.7 103.6 %collective-permute-start.35 = (bf16[128,2048]{1,0:T(8,128)(2,1)S(1)}, bf16[128,2048]{1,0:T(8,128)(2,1)S(1)}, u32[]{:S(2)}, u32[]{:S(2)}) collective-permute-start(bf16[128,2048]{1,0:T(8,128)(2,1)S(1)} %get-tuple-element.70), channel_id=1, source_target_pairs={{0,12},{4,0},{8,4},{12,8},{1,13},{5,1},{9,5},{13,9},{2,14},{6,2},{... | collective-permute-start | bytes 1572872 | tf_op jit(solution)/shard_map/ppermute | solution.py:54
  991.9 104.8 %collective-permute-start.40 = (bf16[4,1024,128]{2,1,0:T(8,128)(2,1)}, bf16[4,1024,128]{2,1,0:T(8,128)(2,1)}, u32[]{:S(2)}, u32[]{:S(2)}) collective-permute-start(bf16[4,1024,128]{2,1,0:T(8,128)(2,1)} %get-tuple-element.65), channel_id=1, source_target_pairs={{0,18},{1,19},{2,16},{3,17},{16,2},{17,3},{18,0},{19,1},{4,22},{5,... | collective-permute-start | bytes 3145736 | tf_op jit(solution)/shard_map/ppermute | solution.py:65
  993.6 103.2 %collective-permute-start.39 = (bf16[4,1024,128]{2,1,0:T(8,128)(2,1)}, bf16[4,1024,128]{2,1,0:T(8,128)(2,1)}, u32[]{:S(2)}, u32[]{:S(2)}) collective-permute-start(bf16[4,1024,128]{2,1,0:T(8,128)(2,1)} %get-tuple-element.66), channel_id=1, source_target_pairs={{0,2},{1,3},{2,0},{3,1},{16,18},{17,19},{18,16},{19,17},{4,6},{5,7... | collective-permute-start | bytes 3145736 | tf_op jit(solution)/shard_map/ppermute | solution.py:65
  1047.4 49.4 %collective-permute-start.38 = (bf16[4,1024,128]{2,1,0:T(8,128)(2,1)}, bf16[4,1024,128]{2,1,0:T(8,128)(2,1)}, u32[]{:S(2)}, u32[]{:S(2)}) collective-permute-start(bf16[4,1024,128]{2,1,0:T(8,128)(2,1)} %get-tuple-element.64), channel_id=1, source_target_pairs={{0,16},{1,17},{2,18},{3,19},{16,0},{17,1},{18,2},{19,3},{4,20},{5,... | collective-permute-start | bytes 3145736 | tf_op jit(solution)/shard_map/ppermute | solution.py:65
  1100.9 51.1 %all-to-all-start.2 = ((bf16[4,1024,128]{2,0,1:T(4,128)(2,1)}), bf16[4,1024,128]{2,0,1:T(4,128)(2,1)S(1)}, u32[]{:S(2)}, u32[]{:S(2)}) async-start(bf16[4,1024,128]{2,0,1:T(4,128)(2,1)} %copy.371), calls=%async_computation.2 | async-start | bytes 2097152 | tf_op jit(solution)/shard_map/all_to_all | solution.py:100
  (97 other events, 2470.4 us)
Sparse Core Ops, SparseCore 0:
  812.9 78.6 all-gather.2
  1093.7 43.1 all-gather.4
where the time goes:
time: 1250 us; the launch traced here: 1240 us
  waiting for transfers between devices  598 us (48%)
  starting transfers between devices  175 us (14%)
  local copies, waits for them, and re-layouts  154 us (12%)
  other arithmetic  139 us (11%)
  matrix products  114 us (9%)
  blocking collectives  40.1 us (3%)
  between operations  19.1 us (2%)
    ppermute x24, waiting for transfers between devices, by_ctx(): lax.ppermute(block, 'ctx', [(i, (i + shift) % n_c) for i in range(n_c)])  370 us
    ppermute x12, waiting for transfers between devices, by_pack(): return lax.ppermute(block, ('fsdp', 'tp'), pairs)  222 us
    ppermute x24, starting transfers between devices, by_ctx(): lax.ppermute(block, 'ctx', [(i, (i + shift) % n_c) for i in range(n_c)])  125 us
    dot_general x21, matrix products, dot(): lax.dot_general(left, right, (dims, ((), ())), preferred_element_type=F32)  95.9 us
    psum x1, blocking collectives, shards(): lax.psum(jnp.sum(att_total * att_total) + jnp.sum(ff_total * ff_total), (...  40.1 us
    dot_general x6, local copies, waits for them, and re-layouts, dot(): lax.dot_general(left, right, (dims, ((), ())), preferred_element_type=F32)  35.6 us
    unnamed x169, local copies, waits for them, and re-layouts  31.6 us
    all_to_all x2, starting transfers between devices, scatter_grad(): return lax.all_to_all(total.astype(BF), 'ctx', 1, 2, tiled=True).astype(F32)  25.3 us
  transfers between devices with their start and end apart: 50, of which 22 were waited for; matrix products, arithmetic and copies ran while one was open for 22% of the time, Pallas kernels for 0%

commit v1 on v0

--- a/solution.py
+++ b/solution.py
@@ -16,6 +16,28 @@
 F32 = jnp.float32
 
 
+def cut_along(x, dim, devices):
+    before, after = (x.shape[:dim], x.shape[dim + 1 :])
+    return jnp.moveaxis(x.reshape(*before, devices, -1, *after), dim, 0)
+
+
+def in_order(blocks, dim):
+    shape = list(blocks.shape[1:])
+    shape[dim] *= blocks.shape[0]
+    return jnp.moveaxis(blocks, 0, dim).reshape(shape)
+
+
+def exchange_directly(value, axis, split_dim, concat_dim):
+    size, mine = (lax.axis_size(axis), lax.axis_index(axis))
+    tiles = cut_along(value, split_dim, size)
+    done = [tiles[mine]]
+    for turn in range(1, size):
+        sent = tiles[(mine + turn) % size]
+        done.append(lax.ppermute(sent, axis, [(i, (i + turn) % size) for i in range(size)]))
+    tiles = jnp.stack(done)[(mine - jnp.arange(size)) % size]
+    return in_order(tiles, concat_dim)
+
+
 def mean_spread(values):
     centre = values - jnp.mean(values, axis=-1, keepdims=True)
     spread = jnp.mean(centre * centre, axis=-1, keepdims=True)
@@ -80,7 +102,7 @@
         return total
 
     def gather_weight(shard):
-        swapped = lax.all_to_all(shard.astype(BF), "ctx", 2, 1, tiled=True)
+        swapped = exchange_directly(shard.astype(BF), "ctx", 2, 1)
         columns = []
         for other in range(2):
             parts = [

time: 1250 us -> 1190 us (0.952)
  waiting for transfers between devices: 598 us -> 533 us
  local copies, waits for them, and re-layouts: 154 us -> 171 us
    ppermute x24, waiting for transfers between devices: 370 us -> 275 us  [by_ctx(): lax.ppermute(block, 'ctx', [(i, (i + shift) % n_c) for i in range(n_c)])]
    ppermute x0 -> x6, waiting for transfers between devices: none -> 58.5 us  [exchange_directly(): lax.ppermute(sent, axis, [(i, (i + turn) % size) for i in range(size)])]
    ppermute x24, starting transfers between devices: 125 us -> 94.9 us  [by_ctx(): lax.ppermute(block, 'ctx', [(i, (i + shift) % n_c) for i in range(n_c)])]
    ppermute x0 -> x6, starting transfers between devices: none -> 28.4 us  [exchange_directly(): lax.ppermute(sent, axis, [(i, (i + turn) % size) for i in range(size)])]
    ppermute x12, waiting for transfers between devices: 222 us -> 199 us  [by_pack(): return lax.ppermute(block, ('fsdp', 'tp'), pairs)]
    unnamed x169 -> x192, local copies, waits for them, and re-layouts: 31.6 us -> 41 us
    another operation x2 -> x10, local copies, waits for them, and re-layouts: 19 us -> 26 us
    dot_general x6 -> x10, local copies, waits for them, and re-layouts: 35.6 us -> 41.6 us  [dot(): lax.dot_general(left, right, (dims, ((), ())), preferred_element_type=F32)]
  transfers between devices with their start and end apart: 50 -> 54, of which waited for: 22 -> 21; matrix products, arithmetic and copies ran while one was open for 22% -> 25% of each run, Pallas kernels for 0% -> 0%
where the time goes in v1:
time: 1190 us; the launch traced here: 1180 us
  waiting for transfers between devices  533 us (45%)
  local copies, waits for them, and re-layouts  171 us (14%)
  starting transfers between devices  164 us (14%)
  other arithmetic  139 us (12%)
  matrix products  119 us (10%)
  blocking collectives  40 us (3%)
  between operations  19.4 us (2%)
    ppermute x24, waiting for transfers between devices, by_ctx(): lax.ppermute(block, 'ctx', [(i, (i + shift) % n_c) for i in range(n_c)])  275 us
    ppermute x12, waiting for transfers between devices, by_pack(): return lax.ppermute(block, ('fsdp', 'tp'), pairs)  199 us
    dot_general x21, matrix products, dot(): lax.dot_general(left, right, (dims, ((), ())), preferred_element_type=F32)  102 us
    ppermute x24, starting transfers between devices, by_ctx(): lax.ppermute(block, 'ctx', [(i, (i + shift) % n_c) for i in range(n_c)])  94.9 us
    ppermute x6, waiting for transfers between devices, exchange_directly(): lax.ppermute(sent, axis, [(i, (i + turn) % size) for i in range(size)])  58.5 us
    dot_general x10, local copies, waits for them, and re-layouts, dot(): lax.dot_general(left, right, (dims, ((), ())), preferred_element_type=F32)  41.6 us
    unnamed x192, local copies, waits for them, and re-layouts  41 us
    psum x1, blocking collectives, shards(): lax.psum(jnp.sum(att_total * att_total) + jnp.sum(ff_total * ff_total), (...  40 us
  transfers between devices with their start and end apart: 54, of which 21 were waited for; matrix products, arithmetic and copies ran while one was open for 25% of the time, Pallas kernels for 0%

profile of v1, /device:TPU:0, one launch (start us, length us, event | category | flops | bytes accessed | tf_op | source)
XLA Modules:
  0.0 1184.8 jit_solution(18328997110236580900)
XLA Ops:
  28.0 22.0 %collective-permute-start.4 = (bf16[4,256,128]{2,1,0:T(8,128)(2,1)S(1)}, bf16[4,256,128]{2,1,0:T(8,128)(2,1)S(1)}, u32[]{:S(2)}, u32[]{:S(2)}) collective-permute-start(bf16[4,256,128]{2,1,0:T(8,128)(2,1)S(1)} %bitcast.562), channel_id=1, source_target_pairs={{0,4},{4,8},{8,12},{12,0},{1,5},{5,9},{9,13},{13,1},{2,6},{6,10},{... | collective-permute-start | bytes 786440 | tf_op jit(solution)/shard_map/ppermute | solution.py:36
  50.0 22.8 %collective-permute-done.1 = bf16[128,2048]{1,0:T(8,128)(2,1)} collective-permute-done((bf16[128,2048]{1,0:T(8,128)(2,1)}, bf16[128,2048]{1,0:T(8,128)(2,1)}, u32[]{:S(2)}, u32[]{:S(2)}) %collective-permute-start.1) | collective-permute-done | bytes 524320 | tf_op jit(solution)/shard_map/ppermute | solution.py:76
  91.2 19.7 %collective-permute-done.9 = bf16[4,1024,128]{2,1,0:T(8,128)(2,1)S(1)} collective-permute-done((bf16[4,1024,128]{2,1,0:T(8,128)(2,1)S(1)}, bf16[4,1024,128]{2,1,0:T(8,128)(2,1)S(1)}, u32[]{:S(2)}, u32[]{:S(2)}) %collective-permute-start.9) | collective-permute-done | bytes 1048608 | tf_op jit(solution)/shard_map/ppermute | solution.py:87
  110.9 20.5 %collective-permute-done.8 = bf16[4,1024,128]{2,1,0:T(8,128)(2,1)} collective-permute-done((bf16[4,1024,128]{2,1,0:T(8,128)(2,1)S(1)}, bf16[4,1024,128]{2,1,0:T(8,128)(2,1)}, u32[]{:S(2)}, u32[]{:S(2)}) %collective-permute-start.8) | collective-permute-done | bytes 1048608 | tf_op jit(solution)/shard_map/ppermute | solution.py:87
  200.9 20.7 %collective-permute-done.29 = bf16[128,2048]{1,0:T(8,128)(2,1)} collective-permute-done((bf16[128,2048]{1,0:T(8,128)(2,1)}, bf16[128,2048]{1,0:T(8,128)(2,1)}, u32[]{:S(2)}, u32[]{:S(2)}) %collective-permute-start.29) | collective-permute-done | bytes 524320 | tf_op jit(solution)/shard_map/ppermute | solution.py:76
  221.6 33.4 %collective-permute-start.12 = (bf16[128,2048]{1,0:T(8,128)(2,1)}, bf16[128,2048]{1,0:T(8,128)(2,1)S(1)}, u32[]{:S(2)}, u32[]{:S(2)}) collective-permute-start(bf16[128,2048]{1,0:T(8,128)(2,1)} %get-tuple-element.93), channel_id=1, source_target_pairs={{0,8},{4,12},{8,0},{12,4},{1,9},{5,13},{9,1},{13,5},{2,10},{6,14},... | collective-permute-start | bytes 1572872 | tf_op jit(solution)/shard_map/ppermute | solution.py:76
  259.2 52.3 %collective-permute-done.19 = bf16[3,256,512]{2,1,0:T(8,128)(2,1)S(1)} collective-permute-done((bf16[3,256,512]{2,1,0:T(8,128)(2,1)}, bf16[3,256,512]{2,1,0:T(8,128)(2,1)S(1)}, u32[]{:S(2)}, u32[]{:S(2)}) %collective-permute-start.19) | collective-permute-done | bytes 786464 | tf_op jit(solution)/shard_map/ppermute | solution.py:36
  325.9 7.7 collective-permute-done.11
  338.1 12.3 %collective-permute-done.16 = bf16[128,2048]{1,0:T(8,128)(2,1)S(1)} collective-permute-done((bf16[128,2048]{1,0:T(8,128)(2,1)S(1)}, bf16[128,2048]{1,0:T(8,128)(2,1)S(1)}, u32[]{:S(2)}, u32[]{:S(2)}) %collective-permute-start.16) | collective-permute-done | bytes 524320 | tf_op jit(solution)/shard_map/ppermute | solution.py:76
  350.4 23.3 %collective-permute-start.14 = (bf16[128,2048]{1,0:T(8,128)(2,1)S(1)}, bf16[128,2048]{1,0:T(8,128)(2,1)S(1)}, u32[]{:S(2)}, u32[]{:S(2)}) collective-permute-start(bf16[128,2048]{1,0:T(8,128)(2,1)S(1)} %fusion.79), channel_id=1, source_target_pairs={{0,4},{4,8},{8,12},{12,0},{1,5},{5,9},{9,13},{13,1},{2,6},{6,10},{... | collective-permute-start | bytes 1572872 | tf_op jit(solution)/shard_map/ppermute | solution.py:76
  378.0 8.2 reshape.641
  386.2 11.2 copy.317
  407.9 53.6 %collective-permute-done.22 = bf16[3,1024,512]{2,1,0:T(8,128)(2,1)} collective-permute-done((bf16[3,1024,512]{2,1,0:T(8,128)(2,1)}, bf16[3,1024,512]{2,1,0:T(8,128)(2,1)}, u32[]{:S(2)}, u32[]{:S(2)}) %collective-permute-start.22) | collective-permute-done | bytes 3145760 | tf_op jit(solution)/shard_map/ppermute | solution.py:87
  461.6 14.6 %maximum_maximum_fusion = bf16[3,2048,1024]{2,1,0:T(8,128)(2,1)S(1)} fusion(bf16[3,1024,512]{2,1,0:T(8,128)(2,1)} %collective-permute-done.23, bf16[3,1024,512]{2,1,0:T(8,128)(2,1)} %collective-permute-done.22, bf16[3,1024,512]{2,1,0:T(8,128)(2,1)} %collective-permute-done.21, bf16[3,1024,512]{2,1,0:T(8,128)(2,1)} %bitcast.71), kind=kLoop, calls=%fused_computation.4 | loop fusion | flops 50331648 | bytes 25165824 | tf_op jit(solution)/shard_map/concatenate | solution.py:112
  494.2 8.1 fusion.22
  504.3 11.1 fusion.12
  526.2 9.3 convolution_convert_fusion.1
  535.5 13.9 %fusion.20 = f32[1024,2048]{1,0:T(8,128)} fusion(bf16[3,2048,1024]{2,1,0:T(8,128)(2,1)} %copy-done.14, f32[1024,1024]{1,0:T(8,128)S(1)} %copy-done.35, f32[1024,1024]{1,0:T(8,128)S(1)} %copy-done.31, f32[1024,1024]{1,0:T(8,128)} %copy.273), kind=kOutput, calls=%fused_computation.66 | convolution fusion | flops 4305453056 | bytes 25165824 | tf_op jit(solution)/shard_map/dot_general | solution.py:57
  549.4 11.6 add_convert_fusion.1
  594.9 9.9 collective-permute-done.35
  604.8 22.3 %collective-permute-done.34 = bf16[128,2048]{1,0:T(8,128)(2,1)} collective-permute-done((bf16[128,2048]{1,0:T(8,128)(2,1)}, bf16[128,2048]{1,0:T(8,128)(2,1)}, u32[]{:S(2)}, u32[]{:S(2)}) %collective-permute-start.34) | collective-permute-done | bytes 524320 | tf_op jit(solution)/shard_map/ppermute | solution.py:76
  629.0 9.5 collective-permute-done.27
  638.5 32.7 %collective-permute-done.26 = bf16[128,2048]{1,0:T(8,128)(2,1)S(1)} collective-permute-done((bf16[128,2048]{1,0:T(8,128)(2,1)S(1)}, bf16[128,2048]{1,0:T(8,128)(2,1)S(1)}, u32[]{:S(2)}, u32[]{:S(2)}) %collective-permute-start.26) | collective-permute-done | bytes 524320 | tf_op jit(solution)/shard_map/ppermute | solution.py:76
  672.0 9.9 collective-permute-start.38
  694.4 34.8 %collective-permute-done.37 = bf16[128,2048]{1,0:T(8,128)(2,1)S(1)} collective-permute-done((bf16[128,2048]{1,0:T(8,128)(2,1)S(1)}, bf16[128,2048]{1,0:T(8,128)(2,1)S(1)}, u32[]{:S(2)}, u32[]{:S(2)}) %collective-permute-start.37) | collective-permute-done | bytes 524320 | tf_op jit(solution)/shard_map/ppermute | solution.py:76
  744.5 12.4 %pad_maximum_fusion = f32[3,2,1024,2,512]{4,2,3,1,0:T(8,128)} fusion(f32[1,2,1024,2,512]{4,2,3,1,0:T(8,128)} %convolution_bitcast_fusion, f32[1,2,1024,2,512]{4,2,3,1,0:T(8,128)S(1)} %convolution_bitcast_fusion.1, f32[1,2,1024,2,512]{4,2,3,1,0:T(8,128)S(1)} %convolution_bitcast_fusion.2), kind=kLoop, calls=%fused_computation.3 | loop fusion | flops 12582912 | bytes 50331648 | tf_op jit(solution)/shard_map/stack | solution.py:235
  785.8 27.3 %collective-permute-done.49 = bf16[3,1024,512]{2,1,0:T(8,128)(2,1)} collective-permute-done((bf16[3,1024,512]{2,1,0:T(8,128)(2,1)}, bf16[3,1024,512]{2,1,0:T(8,128)(2,1)}, u32[]{:S(2)}, u32[]{:S(2)}) %collective-permute-start.49) | collective-permute-done | bytes 3145760 | tf_op jit(solution)/shard_map/ppermute | solution.py:87
  813.1 78.2 %collective-permute-done.48 = bf16[3,1024,512]{2,1,0:T(8,128)(2,1)} collective-permute-done((bf16[3,1024,512]{2,1,0:T(8,128)(2,1)}, bf16[3,1024,512]{2,1,0:T(8,128)(2,1)}, u32[]{:S(2)}, u32[]{:S(2)}) %collective-permute-start.48) | collective-permute-done | bytes 3145760 | tf_op jit(solution)/shard_map/ppermute | solution.py:87
  939.8 52.9 %collective-permute-done.43 = bf16[128,2048]{1,0:T(8,128)(2,1)S(1)} collective-permute-done((bf16[128,2048]{1,0:T(8,128)(2,1)S(1)}, bf16[128,2048]{1,0:T(8,128)(2,1)S(1)}, u32[]{:S(2)}, u32[]{:S(2)}) %collective-permute-start.43) | collective-permute-done | bytes 524320 | tf_op jit(solution)/shard_map/ppermute | solution.py:76
  994.0 42.5 %collective-permute-done.42 = bf16[128,2048]{1,0:T(8,128)(2,1)S(1)} collective-permute-done((bf16[128,2048]{1,0:T(8,128)(2,1)S(1)}, bf16[128,2048]{1,0:T(8,128)(2,1)S(1)}, u32[]{:S(2)}, u32[]{:S(2)}) %collective-permute-start.42) | collective-permute-done | bytes 524320 | tf_op jit(solution)/shard_map/ppermute | solution.py:76
  1046.2 20.4 %all-to-all-start = ((bf16[4,1024,128]{2,0,1:T(4,128)(2,1)}), bf16[4,1024,128]{2,0,1:T(4,128)(2,1)S(1)}, u32[]{:S(2)}, u32[]{:S(2)}) async-start(bf16[4,1024,128]{2,0,1:T(4,128)(2,1)} %copy.298), calls=%async_computation | async-start | bytes 2097152 | tf_op jit(solution)/shard_map/all_to_all | solution.py:122
  1104.0 40.0 %psum.7 = f32[]{:T(128)} all-reduce(f32[]{:T(128)S(6)} %add.503), channel_id=1, replica_groups=mesh['fsdp'=2,'ctx'=4,'tp'=4] {'fsdp','ctx','tp'}, use_global_device_ids=true, to_apply=%region_15.16 | all-reduce | flops 1 | bytes 8 | tf_op jit(solution)/shard_map/psum | solution.py:270
  (423 shorter events, 396.4 us)
Async XLA Ops:
  7.2 1059.4 %all-gather.3.cloned.1.call-start = ((), (), s32[]{:S(2)}) async-start(), calls=%async_computation.2 | async-start | bytes 2621440 | tf_op jit(solution)/shard_map/all_gather | solution.py:234
  15.3 57.5 %collective-permute-start.1 = (bf16[128,2048]{1,0:T(8,128)(2,1)}, bf16[128,2048]{1,0:T(8,128)(2,1)}, u32[]{:S(2)}, u32[]{:S(2)}) collective-permute-start(bf16[128,2048]{1,0:T(8,128)(2,1)} %fusion.49), channel_id=1, source_target_pairs={{0,8},{4,12},{8,0},{12,4},{1,9},{5,13},{9,1},{13,5},{2,10},{6,14},... | collective-permute-start | bytes 1572872 | tf_op jit(solution)/shard_map/ppermute | solution.py:76
  15.3 57.5 %collective-permute-start = (bf16[128,2048]{1,0:T(8,128)(2,1)}, bf16[128,2048]{1,0:T(8,128)(2,1)}, u32[]{:S(2)}, u32[]{:S(2)}) collective-permute-start(bf16[128,2048]{1,0:T(8,128)(2,1)} %fusion.49), channel_id=1, source_target_pairs={{0,4},{4,8},{8,12},{12,0},{1,5},{5,9},{9,13},{13,1},{2,6},{6,10},{... | collective-permute-start | bytes 1572872 | tf_op jit(solution)/shard_map/ppermute | solution.py:76
  18.1 58.4 %collective-permute-start.6 = (bf16[4,256,128]{2,1,0:T(8,128)(2,1)S(1)}, bf16[4,256,128]{2,1,0:T(8,128)(2,1)S(1)}, u32[]{:S(2)}, u32[]{:S(2)}) collective-permute-start(bf16[4,256,128]{2,1,0:T(8,128)(2,1)S(1)} %bitcast.560), channel_id=1, source_target_pairs={{0,12},{4,0},{8,4},{12,8},{1,13},{5,1},{9,5},{13,9},{2,14},{6,2},{... | collective-permute-start | bytes 786440 | tf_op jit(solution)/shard_map/ppermute | solution.py:36
  21.2 61.6 %collective-permute-start.5 = (bf16[4,256,128]{2,1,0:T(8,128)(2,1)S(1)}, bf16[4,256,128]{2,1,0:T(8,128)(2,1)S(1)}, u32[]{:S(2)}, u32[]{:S(2)}) collective-permute-start(bf16[4,256,128]{2,1,0:T(8,128)(2,1)S(1)} %bitcast.561), channel_id=1, source_target_pairs={{0,8},{4,12},{8,0},{12,4},{1,9},{5,13},{9,1},{13,5},{2,10},{6,14},... | collective-permute-start | bytes 786440 | tf_op jit(solution)/shard_map/ppermute | solution.py:36
  28.0 54.8 %collective-permute-start.4 = (bf16[4,256,128]{2,1,0:T(8,128)(2,1)S(1)}, bf16[4,256,128]{2,1,0:T(8,128)(2,1)S(1)}, u32[]{:S(2)}, u32[]{:S(2)}) collective-permute-start(bf16[4,256,128]{2,1,0:T(8,128)(2,1)S(1)} %bitcast.562), channel_id=1, source_target_pairs={{0,4},{4,8},{8,12},{12,0},{1,5},{5,9},{9,13},{13,1},{2,6},{6,10},{... | collective-permute-start | bytes 786440 | tf_op jit(solution)/shard_map/ppermute | solution.py:36
  76.5 65.0 %collective-permute-start.3 = (bf16[4,128,2048]{2,1,0:T(8,128)(2,1)}, bf16[4,128,2048]{2,1,0:T(8,128)(2,1)}, u32[]{:S(2)}, u32[]{:S(2)}) collective-permute-start(bf16[4,128,2048]{2,1,0:T(8,128)(2,1)} %get-tuple-element.95), channel_id=1, source_target_pairs={{0,1},{1,0},{2,3},{3,2},{4,5},{5,4},{6,7},{7,6},{8,9},{9,8},{10,11... | collective-permute-start | bytes 6291464 | tf_op jit(solution)/shard_map/ppermute | solution.py:79
  188.3 66.7 %collective-permute-start.20 = (bf16[3,256,512]{2,1,0:T(8,128)(2,1)}, bf16[3,256,512]{2,1,0:T(8,128)(2,1)}, u32[]{:S(2)}, u32[]{:S(2)}) collective-permute-start(bf16[3,256,512]{2,1,0:T(8,128)(2,1)} %bitcast.68), channel_id=1, source_target_pairs={{0,12},{4,0},{8,4},{12,8},{1,13},{5,1},{9,5},{13,9},{2,14},{6,2},{... | collective-permute-start | bytes 2359304 | tf_op jit(solution)/shard_map/ppermute | solution.py:36
  193.9 117.5 %collective-permute-start.19 = (bf16[3,256,512]{2,1,0:T(8,128)(2,1)}, bf16[3,256,512]{2,1,0:T(8,128)(2,1)S(1)}, u32[]{:S(2)}, u32[]{:S(2)}) collective-permute-start(bf16[3,256,512]{2,1,0:T(8,128)(2,1)} %bitcast.552), channel_id=1, source_target_pairs={{0,8},{4,12},{8,0},{12,4},{1,9},{5,13},{9,1},{13,5},{2,10},{6,14},... | collective-permute-start | bytes 2359304 | tf_op jit(solution)/shard_map/ppermute | solution.py:36
  194.0 117.4 %collective-permute-start.18 = (bf16[3,256,512]{2,1,0:T(8,128)(2,1)}, bf16[3,256,512]{2,1,0:T(8,128)(2,1)S(1)}, u32[]{:S(2)}, u32[]{:S(2)}) collective-permute-start(bf16[3,256,512]{2,1,0:T(8,128)(2,1)} %bitcast.551), channel_id=1, source_target_pairs={{0,4},{4,8},{8,12},{12,0},{1,5},{5,9},{9,13},{13,1},{2,6},{6,10},{... | collective-permute-start | bytes 2359304 | tf_op jit(solution)/shard_map/ppermute | solution.py:36
  221.5 102.5 %collective-permute-start.13 = (bf16[128,2048]{1,0:T(8,128)(2,1)}, bf16[128,2048]{1,0:T(8,128)(2,1)S(1)}, u32[]{:S(2)}, u32[]{:S(2)}) collective-permute-start(bf16[128,2048]{1,0:T(8,128)(2,1)} %get-tuple-element.92), channel_id=1, source_target_pairs={{0,4},{4,8},{8,12},{12,0},{1,5},{5,9},{9,13},{13,1},{2,6},{6,10},{... | collective-permute-start | bytes 1572872 | tf_op jit(solution)/shard_map/ppermute | solution.py:76
  221.6 103.8 %collective-permute-start.12 = (bf16[128,2048]{1,0:T(8,128)(2,1)}, bf16[128,2048]{1,0:T(8,128)(2,1)S(1)}, u32[]{:S(2)}, u32[]{:S(2)}) collective-permute-start(bf16[128,2048]{1,0:T(8,128)(2,1)} %get-tuple-element.93), channel_id=1, source_target_pairs={{0,8},{4,12},{8,0},{12,4},{1,9},{5,13},{9,1},{13,5},{2,10},{6,14},... | collective-permute-start | bytes 1572872 | tf_op jit(solution)/shard_map/ppermute | solution.py:76
  255.0 78.6 %collective-permute-start.11 = (bf16[128,2048]{1,0:T(8,128)(2,1)}, bf16[128,2048]{1,0:T(8,128)(2,1)S(1)}, u32[]{:S(2)}, u32[]{:S(2)}) collective-permute-start(bf16[128,2048]{1,0:T(8,128)(2,1)} %get-tuple-element.91), channel_id=1, source_target_pairs={{0,12},{4,0},{8,4},{12,8},{1,13},{5,1},{9,5},{13,9},{2,14},{6,2},{... | collective-permute-start | bytes 1572872 | tf_op jit(solution)/shard_map/ppermute | solution.py:76
  322.4 85.5 %collective-permute-start.23 = (bf16[3,1024,512]{2,1,0:T(8,128)(2,1)}, bf16[3,1024,512]{2,1,0:T(8,128)(2,1)}, u32[]{:S(2)}, u32[]{:S(2)}) collective-permute-start(bf16[3,1024,512]{2,1,0:T(8,128)(2,1)} %bitcast.71), channel_id=1, source_target_pairs={{0,18},{1,19},{2,16},{3,17},{16,2},{17,3},{18,0},{19,1},{4,22},{5,... | collective-permute-start | bytes 9437192 | tf_op jit(solution)/shard_map/ppermute | solution.py:87
  324.1 137.5 %collective-permute-start.22 = (bf16[3,1024,512]{2,1,0:T(8,128)(2,1)}, bf16[3,1024,512]{2,1,0:T(8,128)(2,1)}, u32[]{:S(2)}, u32[]{:S(2)}) collective-permute-start(bf16[3,1024,512]{2,1,0:T(8,128)(2,1)} %bitcast.71), channel_id=1, source_target_pairs={{0,2},{1,3},{2,0},{3,1},{16,18},{17,19},{18,16},{19,17},{4,6},{5,7... | collective-permute-start | bytes 9437192 | tf_op jit(solution)/shard_map/ppermute | solution.py:87
  325.4 136.2 %collective-permute-start.21 = (bf16[3,1024,512]{2,1,0:T(8,128)(2,1)}, bf16[3,1024,512]{2,1,0:T(8,128)(2,1)}, u32[]{:S(2)}, u32[]{:S(2)}) collective-permute-start(bf16[3,1024,512]{2,1,0:T(8,128)(2,1)} %bitcast.71), channel_id=1, source_target_pairs={{0,16},{1,17},{2,18},{3,19},{16,0},{17,1},{18,2},{19,3},{4,20},{5,... | collective-permute-start | bytes 9437192 | tf_op jit(solution)/shard_map/ppermute | solution.py:87
  338.1 65.8 %collective-permute-start.15 = (bf16[128,2048]{1,0:T(8,128)(2,1)S(1)}, bf16[128,2048]{1,0:T(8,128)(2,1)S(1)}, u32[]{:S(2)}, u32[]{:S(2)}) collective-permute-start(bf16[128,2048]{1,0:T(8,128)(2,1)S(1)} %fusion.79), channel_id=1, source_target_pairs={{0,8},{4,12},{8,0},{12,4},{1,9},{5,13},{9,1},{13,5},{2,10},{6,14},... | collective-permute-start | bytes 1572872 | tf_op jit(solution)/shard_map/ppermute | solution.py:76
  350.4 53.5 %collective-permute-start.14 = (bf16[128,2048]{1,0:T(8,128)(2,1)S(1)}, bf16[128,2048]{1,0:T(8,128)(2,1)S(1)}, u32[]{:S(2)}, u32[]{:S(2)}) collective-permute-start(bf16[128,2048]{1,0:T(8,128)(2,1)S(1)} %fusion.79), channel_id=1, source_target_pairs={{0,4},{4,8},{8,12},{12,0},{1,5},{5,9},{9,13},{13,1},{2,6},{6,10},{... | collective-permute-start | bytes 1572872 | tf_op jit(solution)/shard_map/ppermute | solution.py:76
  407.9 84.2 %collective-permute-start.17 = (bf16[4,128,2048]{2,1,0:T(8,128)(2,1)}, bf16[4,128,2048]{2,1,0:T(8,128)(2,1)}, u32[]{:S(2)}, u32[]{:S(2)}) collective-permute-start(bf16[4,128,2048]{2,1,0:T(8,128)(2,1)} %get-tuple-element.90), channel_id=1, source_target_pairs={{0,1},{1,0},{2,3},{3,2},{4,5},{5,4},{6,7},{7,6},{8,9},{9,8},{10,11... | collective-permute-start | bytes 6291464 | tf_op jit(solution)/shard_map/ppermute | solution.py:79
  593.4 77.8 %collective-permute-start.26 = (bf16[128,2048]{1,0:T(8,128)(2,1)S(1)}, bf16[128,2048]{1,0:T(8,128)(2,1)S(1)}, u32[]{:S(2)}, u32[]{:S(2)}) collective-permute-start(bf16[128,2048]{1,0:T(8,128)(2,1)S(1)} %get-tuple-element.88), channel_id=1, source_target_pairs={{0,8},{4,12},{8,0},{12,4},{1,9},{5,13},{9,1},{13,5},{2,10},{6,14},... | collective-permute-start | bytes 1572872 | tf_op jit(solution)/shard_map/ppermute | solution.py:76
  604.8 66.4 %collective-permute-start.25 = (bf16[128,2048]{1,0:T(8,128)(2,1)S(1)}, bf16[128,2048]{1,0:T(8,128)(2,1)S(1)}, u32[]{:S(2)}, u32[]{:S(2)}) collective-permute-start(bf16[128,2048]{1,0:T(8,128)(2,1)S(1)} %get-tuple-element.86), channel_id=1, source_target_pairs={{0,12},{4,0},{8,4},{12,8},{1,13},{5,1},{9,5},{13,9},{2,14},{6,2},{... | collective-permute-start | bytes 1572872 | tf_op jit(solution)/shard_map/ppermute | solution.py:76
  741.0 72.2 %collective-permute-start.49 = (bf16[3,1024,512]{2,1,0:T(8,128)(2,1)}, bf16[3,1024,512]{2,1,0:T(8,128)(2,1)}, u32[]{:S(2)}, u32[]{:S(2)}) collective-permute-start(bf16[3,1024,512]{2,1,0:T(8,128)(2,1)} %get-tuple-element.51), channel_id=1, source_target_pairs={{0,18},{1,19},{2,16},{3,17},{16,2},{17,3},{18,0},{19,1},{4,22},{5,... | collective-permute-start | bytes 9437192 | tf_op jit(solution)/shard_map/ppermute | solution.py:87
  742.6 148.8 %collective-permute-start.48 = (bf16[3,1024,512]{2,1,0:T(8,128)(2,1)}, bf16[3,1024,512]{2,1,0:T(8,128)(2,1)}, u32[]{:S(2)}, u32[]{:S(2)}) collective-permute-start(bf16[3,1024,512]{2,1,0:T(8,128)(2,1)} %get-tuple-element.52), channel_id=1, source_target_pairs={{0,2},{1,3},{2,0},{3,1},{16,18},{17,19},{18,16},{19,17},{4,6},{5,7... | collective-permute-start | bytes 9437192 | tf_op jit(solution)/shard_map/ppermute | solution.py:87
  743.8 147.6 %collective-permute-start.47 = (bf16[3,1024,512]{2,1,0:T(8,128)(2,1)}, bf16[3,1024,512]{2,1,0:T(8,128)(2,1)}, u32[]{:S(2)}, u32[]{:S(2)}) collective-permute-start(bf16[3,1024,512]{2,1,0:T(8,128)(2,1)} %get-tuple-element.50), channel_id=1, source_target_pairs={{0,16},{1,17},{2,18},{3,19},{16,0},{17,1},{18,2},{19,3},{4,20},{5,... | collective-permute-start | bytes 9437192 | tf_op jit(solution)/shard_map/ppermute | solution.py:87
  785.8 139.2 %collective-permute-start.40 = (bf16[4,128,2048]{2,1,0:T(8,128)(2,1)}, bf16[4,128,2048]{2,1,0:T(8,128)(2,1)}, u32[]{:S(2)}, u32[]{:S(2)}) collective-permute-start(bf16[4,128,2048]{2,1,0:T(8,128)(2,1)} %slice_bitcast_fusion.14), channel_id=1, source_target_pairs={{0,1},{1,0},{2,3},{3,2},{4,5},{5,4},{6,7},{7,6},{8,9},{9,8},{10,11... | collective-permute-start | bytes 6291464 | tf_op jit(solution)/shard_map/ppermute | solution.py:79
  903.5 142.6 %all-to-all-start.1 = ((bf16[3,1024,512]{2,0,1:T(4,128)(2,1)}), bf16[3,1024,512]{2,0,1:T(4,128)(2,1)}, u32[]{:S(2)}, u32[]{:S(2)}) async-start(bf16[3,1024,512]{2,0,1:T(4,128)(2,1)} %copy.304), calls=%async_computation.1 | async-start | bytes 8388608 | tf_op jit(solution)/shard_map/all_to_all | solution.py:122
  908.4 263.2 %all-gather.5.cloned.1.call-start = ((), (), s32[]{:S(2)}) async-start(), calls=%async_computation.3 | async-start | bytes 5242880 | tf_op jit(solution)/shard_map/all_gather | solution.py:264
  928.4 64.2 %collective-permute-start.43 = (bf16[128,2048]{1,0:T(8,128)(2,1)S(1)}, bf16[128,2048]{1,0:T(8,128)(2,1)S(1)}, u32[]{:S(2)}, u32[]{:S(2)}) collective-permute-start(bf16[128,2048]{1,0:T(8,128)(2,1)S(1)} %get-tuple-element.75), channel_id=1, source_target_pairs={{0,4},{4,8},{8,12},{12,0},{1,5},{5,9},{9,13},{13,1},{2,6},{6,10},{... | collective-permute-start | bytes 1572872 | tf_op jit(solution)/shard_map/ppermute | solution.py:76
  930.4 106.1 %collective-permute-start.42 = (bf16[128,2048]{1,0:T(8,128)(2,1)S(1)}, bf16[128,2048]{1,0:T(8,128)(2,1)S(1)}, u32[]{:S(2)}, u32[]{:S(2)}) collective-permute-start(bf16[128,2048]{1,0:T(8,128)(2,1)S(1)} %get-tuple-element.76), channel_id=1, source_target_pairs={{0,8},{4,12},{8,0},{12,4},{1,9},{5,13},{9,1},{13,5},{2,10},{6,14},... | collective-permute-start | bytes 1572872 | tf_op jit(solution)/shard_map/ppermute | solution.py:76
  932.8 103.8 %collective-permute-start.41 = (bf16[128,2048]{1,0:T(8,128)(2,1)S(1)}, bf16[128,2048]{1,0:T(8,128)(2,1)S(1)}, u32[]{:S(2)}, u32[]{:S(2)}) collective-permute-start(bf16[128,2048]{1,0:T(8,128)(2,1)S(1)} %get-tuple-element.74), channel_id=1, source_target_pairs={{0,12},{4,0},{8,4},{12,8},{1,13},{5,1},{9,5},{13,9},{2,14},{6,2},{... | collective-permute-start | bytes 1572872 | tf_op jit(solution)/shard_map/ppermute | solution.py:76
  937.0 105.0 %collective-permute-start.46 = (bf16[4,1024,128]{2,1,0:T(8,128)(2,1)}, bf16[4,1024,128]{2,1,0:T(8,128)(2,1)}, u32[]{:S(2)}, u32[]{:S(2)}) collective-permute-start(bf16[4,1024,128]{2,1,0:T(8,128)(2,1)} %get-tuple-element.65), channel_id=1, source_target_pairs={{0,18},{1,19},{2,16},{3,17},{16,2},{17,3},{18,0},{19,1},{4,22},{5,... | collective-permute-start | bytes 3145736 | tf_op jit(solution)/shard_map/ppermute | solution.py:87
  938.5 103.5 %collective-permute-start.45 = (bf16[4,1024,128]{2,1,0:T(8,128)(2,1)}, bf16[4,1024,128]{2,1,0:T(8,128)(2,1)}, u32[]{:S(2)}, u32[]{:S(2)}) collective-permute-start(bf16[4,1024,128]{2,1,0:T(8,128)(2,1)} %get-tuple-element.66), channel_id=1, source_target_pairs={{0,2},{1,3},{2,0},{3,1},{16,18},{17,19},{18,16},{19,17},{4,6},{5,7... | collective-permute-start | bytes 3145736 | tf_op jit(solution)/shard_map/ppermute | solution.py:87
  (111 other events, 2747.8 us)
Sparse Core Ops, SparseCore 0:
  757.9 78.7 all-gather.2
  1039.0 43.0 all-gather.4
